TPU v7x, 32 devices: a whole 2x2x4 slice. The times are simulated.
32 devices in a mesh: dp: 8 (over z, y), mp: 4 (over x, core).
Axes of the slice: x: 2, y: 2, z: 4, core: 2. Of those that a mesh axis runs over, the one named last changes fastest.
Arguments:
- tokens: bfloat16 [16384, 1024], P(('dp', 'mp')), may hold values from -6 to 6
- segment_ids: int32 [16384], P(('dp', 'mp')), may hold values from 0 to 63, never falling along the last dimension, each value on 1 to 512 neighbouring positions
- w_qkv: bfloat16 [3, 1024, 1024], P(None, None, 'mp'), may hold values from -0.1875 to 0.1875
- b_qv: bfloat16 [2, 1024], P(None, 'mp'), may hold values from -1.75 to 1.75
- w_out: bfloat16 [1024, 1024], P('mp'), may hold values from -2 to 2
- b_out: bfloat16 [1024], replicated, may hold values from -1.75 to 1.75
- w_up: bfloat16 [1024, 4096], P(None, 'mp'), may hold values from -0.1875 to 0.1875
- b_up: bfloat16 [4096], P('mp'), may hold values from -1.75 to 1.75
- w_down: bfloat16 [4096, 1024], P('mp'), may hold values from -0.125 to 0.125
- b_down: bfloat16 [1024], replicated, may hold values from -1.75 to 1.75
- ln_gain: float32 [2, 1024], replicated, may hold values from 0.5 to 1.5
- ln_bias: float32 [2, 1024], replicated, may hold values from -1.75 to 1.75
- out_grad: bfloat16 [16384, 1024], P(('dp', 'mp')), may hold values from -6 to 6
Outputs:
- block_out: bfloat16 [16384, 1024], P(('dp', 'mp'))
- grad_in: float32 [16384, 1024], P(('dp', 'mp'))
- grad_qkv: float32 [3, 1024, 1024], P(None, None, 'mp')
- grad_bqv: float32 [2, 1024], P(None, 'mp')
- grad_wout: float32 [1024, 1024], P('mp')
- grad_bout: float32 [1024], replicated
- grad_up: float32 [1024, 4096], P(None, 'mp')
- grad_bup: float32 [4096], P('mp')
- grad_down: float32 [4096, 1024], P('mp')
- grad_bdown: float32 [1024], replicated
- grad_gain: float32 [2, 1024], replicated
- grad_shift: float32 [2, 1024], replicated
Inputs may be any that keep to these rules, and one draw needn't show every extreme that they name: `segment_ids`: along all frames in order, segment numbers never fall; each segment covers 1 to 512 frames and one covers exactly 512; attention never crosses a row of 1024 frames.
All inputs are finite; a program needn't handle non-finite values.
Results may differ from a plain program's by a relative error of at most 0.02.
Values may be sent and summed in bfloat16 or wider, within the bound.
No kernel may reach another device: no remote copies, remote signals or barrier semaphores. Data moves between devices by JAX's collectives and lax.ppermute only.
A program may use at most 192 MiB of HBM per device.

v0:
```python
import jax
import jax.numpy as jnp
from jax import lax
from jax.sharding import PartitionSpec as P

HD = 64
LEN = 1024
QBLK = 512
EPS = 1e-05


def norm_rows(values, gain, shift):
    center = values - jnp.mean(values, axis=-1, keepdims=True)
    spread = jnp.mean(center * center, axis=-1, keepdims=True)
    return center * lax.rsqrt(spread + EPS) * gain + shift


def split_heads(flat, rows):
    return flat.reshape(rows, LEN, flat.shape[1] // HD, HD)


def block_scores(query, keys, seg_q, seg_k, offset):
    scores = jnp.einsum(
        "rqhd,rkhd->rhqk", query, keys, preferred_element_type=jnp.float32
    ) * HD ** (-0.5)
    q_pos = offset + jnp.arange(query.shape[1], dtype=jnp.int32)
    k_pos = jnp.arange(keys.shape[1], dtype=jnp.int32)
    allowed = (seg_q[:, :, None] == seg_k[:, None, :]) & (
        k_pos[None, None, :] <= q_pos[None, :, None]
    )
    return jnp.where(allowed[:, None], scores, -1e30)


def attention_forward(query, keys, values, seg_all):
    rows = query.shape[0] // LEN
    q4 = split_heads(query, rows)
    k4 = split_heads(keys, rows)
    v4 = split_heads(values, rows)
    seg2 = seg_all.reshape(rows, LEN)
    outputs = []
    totals = []
    for block in range(LEN // QBLK):
        first = block * QBLK
        end = first + QBLK
        scores = block_scores(
            q4[:, first:end], k4[:, :end], seg2[:, first:end], seg2[:, :end], first
        )
        top = jnp.max(scores, axis=-1, keepdims=True)
        expd = jnp.exp(scores - top)
        summed = jnp.sum(expd, axis=-1, keepdims=True)
        weights = (expd / summed).astype(jnp.bfloat16)
        outputs.append(
            jnp.einsum("rhqk,rkhd->rqhd", weights, v4[:, :end], preferred_element_type=jnp.float32)
        )
        totals.append(top + jnp.log(summed))
    attended = jnp.concatenate(outputs, axis=1).reshape(query.shape).astype(jnp.bfloat16)
    return (attended, totals)


def attention_backward(query, keys, values, seg_all, totals, grad_att):
    rows = query.shape[0] // LEN
    q4 = split_heads(query, rows)
    k4 = split_heads(keys, rows)
    v4 = split_heads(values, rows)
    g4 = split_heads(grad_att, rows)
    seg2 = seg_all.reshape(rows, LEN)
    scale = HD ** (-0.5)
    grad_k = jnp.zeros(k4.shape, jnp.float32)
    grad_v = jnp.zeros(v4.shape, jnp.float32)
    grad_q_parts = []
    for block in range(LEN // QBLK):
        first = block * QBLK
        end = first + QBLK
        scores = block_scores(
            q4[:, first:end], k4[:, :end], seg2[:, first:end], seg2[:, :end], first
        )
        probs = jnp.exp(scores - totals[block])
        weights = probs.astype(jnp.bfloat16)
        grad_w = jnp.einsum(
            "rqhd,rkhd->rhqk", g4[:, first:end], v4[:, :end], preferred_element_type=jnp.float32
        )
        delta = jnp.sum(probs * grad_w, axis=-1, keepdims=True)
        grad_s = (probs * (grad_w - delta)).astype(jnp.bfloat16)
        grad_q_parts.append(
            jnp.einsum("rhqk,rkhd->rqhd", grad_s, k4[:, :end], preferred_element_type=jnp.float32)
            * scale
        )
        padding = ((0, 0), (0, LEN - end), (0, 0), (0, 0))
        grad_k = grad_k + jnp.pad(
            jnp.einsum(
                "rhqk,rqhd->rkhd", grad_s, q4[:, first:end], preferred_element_type=jnp.float32
            )
            * scale,
            padding,
        )
        grad_v = grad_v + jnp.pad(
            jnp.einsum(
                "rhqk,rqhd->rkhd", weights, g4[:, first:end], preferred_element_type=jnp.float32
            ),
            padding,
        )
    shape = query.shape
    grad_q = jnp.concatenate(grad_q_parts, axis=1).reshape(shape).astype(jnp.bfloat16)
    return (
        grad_q,
        grad_k.reshape(shape).astype(jnp.bfloat16),
        grad_v.reshape(shape).astype(jnp.bfloat16),
    )


def shards(
    tokens,
    segment_ids,
    w_qkv,
    b_qv,
    w_out,
    b_out,
    w_up,
    b_up,
    w_down,
    b_down,
    ln_gain,
    ln_bias,
    out_grad,
):
    resid = tokens.astype(jnp.float32)
    qv_bias = b_qv.astype(jnp.float32)
    up_bias = b_up.astype(jnp.float32)
    local_rows = tokens.shape[0]
    normed, first_back = jax.vjp(norm_rows, resid, ln_gain[0], ln_bias[0])
    lowered = normed.astype(jnp.bfloat16)
    joined, seg_all = (
        lax.all_gather(lowered, "mp", axis=0, tiled=True),
        lax.all_gather(segment_ids, "mp", axis=0, tiled=True),
    )
    query = (jnp.dot(joined, w_qkv[0], preferred_element_type=jnp.float32) + qv_bias[0]).astype(
        jnp.bfloat16
    )
    keys = jnp.dot(joined, w_qkv[1], preferred_element_type=jnp.float32).astype(jnp.bfloat16)
    values = (jnp.dot(joined, w_qkv[2], preferred_element_type=jnp.float32) + qv_bias[1]).astype(
        jnp.bfloat16
    )
    query, keys, values = (query, keys, values)
    attended, totals = attention_forward(query, keys, values, seg_all)
    attn_sum = lax.psum_scatter(
        jnp.dot(attended, w_out, preferred_element_type=jnp.float32).astype(jnp.bfloat16),
        "mp",
        scatter_dimension=0,
        tiled=True,
    ).astype(jnp.float32)
    mixed = resid + attn_sum + b_out.astype(jnp.float32)
    normed2, second_back = jax.vjp(norm_rows, mixed, ln_gain[1], ln_bias[1])
    lowered2 = normed2.astype(jnp.bfloat16)
    joined2 = lax.all_gather(lowered2, "mp", axis=0, tiled=True)
    pre_act = jnp.dot(joined2, w_up, preferred_element_type=jnp.float32) + up_bias
    pre_act, activ = (pre_act, jax.nn.gelu(pre_act, approximate=False).astype(jnp.bfloat16))
    block_out = (
        mixed
        + lax.psum_scatter(
            jnp.dot(activ, w_down, preferred_element_type=jnp.float32).astype(jnp.bfloat16),
            "mp",
            scatter_dimension=0,
            tiled=True,
        ).astype(jnp.float32)
        + b_down.astype(jnp.float32)
    ).astype(jnp.bfloat16)
    grad_y = out_grad.astype(jnp.float32)
    grad_z = lax.all_gather(out_grad, "mp", axis=0, tiled=True)
    grad_down = jnp.einsum("tf,td->fd", activ, grad_z, preferred_element_type=jnp.float32)
    grad_bdown = jnp.sum(grad_z, axis=0, dtype=jnp.float32)
    grad_act = jnp.einsum("td,fd->tf", grad_z, w_down, preferred_element_type=jnp.float32)
    gelu_back = jax.vjp(lambda value: jax.nn.gelu(value, approximate=False), pre_act)[1]
    grad_pre = gelu_back(grad_act)[0].astype(jnp.bfloat16)
    grad_up = jnp.einsum("td,tf->df", joined2, grad_pre, preferred_element_type=jnp.float32)
    grad_bup = jnp.sum(grad_pre, axis=0, dtype=jnp.float32)
    grad_n2 = lax.psum_scatter(
        jnp.einsum("tf,df->td", grad_pre, w_up, preferred_element_type=jnp.float32).astype(
            jnp.bfloat16
        ),
        "mp",
        scatter_dimension=0,
        tiled=True,
    ).astype(jnp.float32)
    grad_h, grad_g2, grad_s2 = second_back(grad_n2)
    grad_h = grad_h + grad_y
    grad_branch = lax.all_gather(grad_h.astype(jnp.bfloat16), "mp", axis=0, tiled=True)
    grad_wout = jnp.einsum("tc,td->cd", attended, grad_branch, preferred_element_type=jnp.float32)
    grad_bout = jnp.sum(grad_branch, axis=0, dtype=jnp.float32)
    grad_att = jnp.einsum(
        "td,cd->tc", grad_branch, w_out, preferred_element_type=jnp.float32
    ).astype(jnp.bfloat16)
    grad_q, grad_k, grad_v = attention_backward(query, keys, values, seg_all, totals, grad_att)
    grad_qkv = jnp.stack(
        [
            jnp.einsum("td,tc->dc", joined, piece, preferred_element_type=jnp.float32)
            for piece in (grad_q, grad_k, grad_v)
        ]
    )
    grad_bqv = jnp.stack(
        [jnp.sum(grad_q, axis=0, dtype=jnp.float32), jnp.sum(grad_v, axis=0, dtype=jnp.float32)]
    )
    summed = jnp.zeros((local_rows * lax.axis_size("mp"), w_qkv.shape[1]), jnp.float32)
    for index, piece in enumerate((grad_q, grad_k, grad_v)):
        summed = summed + jnp.einsum(
            "tc,dc->td", piece, w_qkv[index], preferred_element_type=jnp.float32
        )
    grad_n1 = lax.psum_scatter(
        summed.astype(jnp.bfloat16), "mp", scatter_dimension=0, tiled=True
    ).astype(jnp.float32)
    grad_x, grad_g1, grad_s1 = first_back(grad_n1)
    grad_in = grad_x + grad_h
    weight_totals = (
        lax.psum(grad_qkv.astype(jnp.bfloat16), "dp").astype(jnp.float32),
        lax.psum(grad_bqv.astype(jnp.bfloat16), "dp").astype(jnp.float32),
        lax.psum(grad_wout.astype(jnp.bfloat16), "dp").astype(jnp.float32),
        lax.psum(grad_bout.astype(jnp.bfloat16), "dp").astype(jnp.float32),
        lax.psum(grad_up.astype(jnp.bfloat16), "dp").astype(jnp.float32),
        lax.psum(grad_bup.astype(jnp.bfloat16), "dp").astype(jnp.float32),
        lax.psum(grad_down.astype(jnp.bfloat16), "dp").astype(jnp.float32),
        lax.psum(grad_bdown.astype(jnp.bfloat16), "dp").astype(jnp.float32),
    )
    norm_totals = lax.psum(
        (jnp.stack([grad_g1, grad_g2]), jnp.stack([grad_s1, grad_s2])), ("dp", "mp")
    )
    return (block_out, grad_in) + tuple(weight_totals) + tuple(norm_totals)


def solution(mesh):
    in_specs = (
        P(("dp", "mp"), None),
        P(("dp", "mp")),
        P(None, None, "mp"),
        P(None, "mp"),
        P("mp", None),
        P(),
        P(None, "mp"),
        P("mp"),
        P("mp", None),
        P(),
        P(),
        P(),
        P(("dp", "mp"), None),
    )
    out_specs = (
        P(("dp", "mp"), None),
        P(("dp", "mp"), None),
        P(None, None, "mp"),
        P(None, "mp"),
        P("mp", None),
        P(),
        P(None, "mp"),
        P("mp"),
        P("mp", None),
        P(),
        P(),
        P(),
    )
    return jax.shard_map(shards, mesh=mesh, in_specs=in_specs, out_specs=out_specs, check_vma=False)
```

profile of v0, /device:TPU:0, one launch (start us, length us, event | category | flops | bytes accessed | tf_op | source)
XLA Modules:
  0.0 795.8 jit_solution(3557118762227939732)
XLA Ops:
  15.4 6.2 all-gather
  25.2 27.5 %all-gather.6.cloned.1.call-done = bf16[2048,1024]{1,0:T(8,128)(2,1)} async-done(((bf16[512,1024]{1,0:T(8,128)(2,1)}), bf16[2048,1024]{1,0:T(8,128)(2,1)}) %all-gather.6.cloned.1.call-update) | async-done | bytes 4194320 | tf_op jit(solution)/shard_map/all_gather | solution.py:133
  52.7 3.6 fusion.22
  58.2 4.0 copy.62
  62.3 3.6 fusion.23
  100.2 4.0 fusion.55
  110.7 44.1 %reduce-scatter.5.cloned.1.call-done = bf16[512,1024]{1,0:T(8,128)(2,1)} async-done(((bf16[2048,1024]{1,0:T(8,128)(2,1)}), bf16[512,1024]{1,0:T(8,128)(2,1)}) %reduce-scatter.5.cloned.1.call-update) | async-done | bytes 1048592 | tf_op jit(solution)/shard_map/reduce_scatter | solution.py:145
  160.6 34.0 %all-gather.8.cloned.1.call-done = bf16[2048,1024]{1,0:T(8,128)(2,1)} async-done(((bf16[512,1024]{1,0:T(8,128)(2,1)}), bf16[2048,1024]{1,0:T(8,128)(2,1)}) %all-gather.8.cloned.1.call-update) | async-done | bytes 4194320 | tf_op jit(solution)/shard_map/all_gather | solution.py:154
  194.6 11.3 %fusion.91 = f32[2048,1024]{1,0:T(8,128)} fusion(bf16[2048,1024]{1,0:T(8,128)(2,1)} %all-gather.8.cloned.1.call-done, bf16[1024,1024]{1,0:T(8,128)(2,1)} %param.19), kind=kOutput, calls=%fused_computation.163 | convolution fusion | flops 4294967296 | bytes 14680064 | tf_op jit(solution)/shard_map/dot_general | solution.py:155
  205.9 24.6 %all-gather.10.cloned.1.call-done = bf16[2048,1024]{1,0:T(8,128)(2,1)} async-done(((bf16[512,1024]{1,0:T(8,128)(2,1)}), bf16[2048,1024]{1,0:T(8,128)(2,1)}) %all-gather.10.cloned.1.call-update) | async-done | bytes 4194320 | tf_op jit(solution)/shard_map/all_gather | solution.py:168
  230.5 27.5 %fusion.78 = (bf16[1024]{0:T(1024)(128)(2,1)S(1)}, bf16[2048,1024]{1,0:T(8,128)(2,1)S(1)}, f32[2048,1024]{1,0:T(8,128)}) fusion(f32[2048,1024]{1,0:T(8,128)} %fusion.91, f32[1024]{0:T(1024)S(1)} %convert_element_type.188, bf16[2048,1024]{1,0:T(8,128)(2,1)} %all-gather.10.cloned.1.call-done, bf16[1024,1024]{1,0:T(8,128)(2,1)S(1)} %copy-done), kind=kOutput, calls=%fused_computation.151 | convolution fusion | flops 4450155520 | bytes 27269120 | tf_op jit(solution)/shard_map/td,fd->tf/dot_general | solution.py:171
  260.0 6.2 convolution_convert_fusion.1
  266.3 10.4 %multiply_convert_fusion.2 = bf16[2048,1024]{1,0:T(8,128)(2,1)} fusion(f32[2048,1024]{1,0:T(8,128)} %get-tuple-element.31, f32[2048,1024]{1,0:T(8,128)} %fusion.91, f32[1024]{0:T(1024)S(1)} %convert_element_type.188), kind=kLoop, calls=%fused_computation.17 | loop fusion | flops 8388608 | bytes 20975616 | tf_op jit(solution)/shard_map/convert_element_type | solution.py:156
  276.7 8.4 %convolution_convert_fusion.2 = bf16[2048,1024]{1,0:T(8,128)(2,1)} fusion(bf16[2048,1024]{1,0:T(8,128)(2,1)} %multiply_convert_fusion.2, bf16[1024,1024]{1,0:T(8,128)(2,1)S(1)} %copy-done), kind=kOutput, calls=%fused_computation.43 | convolution fusion | flops 4297064448 | bytes 10485760 | tf_op jit(solution)/shard_map/dot_general | solution.py:160
  285.7 25.2 %reduce-scatter.9.cloned.1.call-done = bf16[512,1024]{1,0:T(8,128)(2,1)} async-done(((bf16[2048,1024]{1,0:T(8,128)(2,1)}), bf16[512,1024]{1,0:T(8,128)(2,1)}) %reduce-scatter.9.cloned.1.call-update) | async-done | bytes 1048592 | tf_op jit(solution)/shard_map/reduce_scatter | solution.py:176
  313.3 44.7 %reduce-scatter.7.cloned.1.call-done = bf16[512,1024]{1,0:T(8,128)(2,1)} async-done(((bf16[2048,1024]{1,0:T(8,128)(2,1)}), bf16[512,1024]{1,0:T(8,128)(2,1)}) %reduce-scatter.7.cloned.1.call-update) | async-done | bytes 1048592 | tf_op jit(solution)/shard_map/reduce_scatter | solution.py:159
  358.0 3.7 fusion.81
  364.5 9.5 %convolution_convert_fusion.6 = bf16[1024,1024]{1,0:T(8,128)(2,1)} fusion(bf16[2048,1024]{1,0:T(8,128)(2,1)} %all-gather.8.cloned.1.call-done, bf16[2048,1024]{1,0:T(8,128)(2,1)} %copy-done.55), kind=kOutput, calls=%fused_computation.90 | convolution fusion | flops 4296015872 | bytes 10485760 | tf_op jit(solution)/shard_map/td,tf->df/dot_general | solution.py:174
  374.0 6.0 convolution_convert_fusion.5
  379.9 19.0 %all-gather.12.cloned.1.call-done = bf16[2048,1024]{1,0:T(8,128)(2,1)} async-done(((bf16[512,1024]{1,0:T(8,128)(2,1)}), bf16[2048,1024]{1,0:T(8,128)(2,1)}) %all-gather.12.cloned.1.call-update) | async-done | bytes 4194320 | tf_op jit(solution)/shard_map/all_gather | solution.py:186
  398.9 4.5 convolution_convert_fusion.3
  410.4 5.9 fusion.42
  416.3 4.6 multiply_reduce_fusion.1
  429.7 14.7 %multiply_reduce_fusion = (f32[2,4,512]{2,1,0:T(4,128)S(1)}, f32[2,4,512,1024]{3,2,1,0:T(8,128)}) fusion(f32[2,4,512,1024]{3,2,1,0:T(8,128)} %copy-done.2, f32[2,4,512]{2,1,0:T(4,128)S(1)} %bitcast.140, bf16[2,512,4,64]{1,3,2,0:T(8,128)(2,1)} %copy.98, bf16[2,1024,4,64]{1,3,2,0:T(8,128)(2,1)S(1)} %copy-done.15), kind=kOutput, calls=%fused_computation.1 | convolution fusion | flops 549449728 | bytes 35160064 | tf_op jit(solution)/shard_map/rqhd,rkhd->rhqk/dot_general | solution.py:79
  444.4 7.8 fusion.90
  453.6 10.9 %multiply_convert_fusion = bf16[2,4,512,1024]{3,2,1,0:T(8,128)(2,1)} fusion(f32[2,4,512,1024]{3,2,1,0:T(8,128)} %get-tuple-element.54, f32[2,4,512,1024]{3,2,1,0:T(8,128)S(1)} %bitcast.125, f32[2,4,512]{2,1,0:T(4,128)S(1)} %get-tuple-element.53, f32[2,4,512]{2,1,0:T(4,128)S(1)} %bitcast.142), kind=kLoop, calls=%fused_computation | loop fusion | flops 16777216 | bytes 41975808 | tf_op jit(solution)/shard_map/convert_element_type | solution.py:83
  464.6 6.2 fusion.47
  497.5 23.2 %all-reduce.3 = (bf16[2,256]{1,0:T(2,128)(2,1)S(1)}, bf16[1024]{0:T(1024)(128)(2,1)S(1)}, bf16[1024]{0:T(1024)(128)(2,1)S(1)}, bf16[1024]{0:T(1024)(128)(2,1)S(1)}) all-reduce(bf16[2,256]{1,0:T(2,128)(2,1)S(1)} %pad_maximum_fusion.4, bf16[1024]{0:T(1024)(128)(2,1)S(1)} %reduce_sum.244, ...), channel_id=1, replica_groups=mesh['dp'=8,'mp'=4] {'dp'}, use_global_device_ids=true, to_apply=%region_21.22 | all-reduce | flops 3584 | bytes 14336 | tf_op jit(solution)/shard_map/psum | solution.py:214
  523.1 171.2 %all-reduce.7.cloned.1.call-done = (bf16[3,1024,256]{2,1,0:T(8,128)(2,1)}, bf16[256,1024]{1,0:T(8,128)(2,1)}, bf16[1024,1024]{1,0:T(8,128)(2,1)}, bf16[1024,1024]{1,0:T(8,128)(2,1)}) async-done(((bf16[3,1024,256]{2,1,0:T(8,128)(2,1)}, bf16[256,1024]{1,0:T(8,128)(2,1)}, bf16[1024,1024]{1,0:T(8,128)(2,1)}, bf16[1024,1024]{1,0:T(8,128)(2,1)}), (bf16[3,1024,256]{2,1,0:T(8,128)(2,1)}, ...) | async-done | bytes 6291472 | tf_op jit(solution)/shard_map/psum | solution.py:213
  705.4 35.1 %reduce-scatter.11.cloned.1.call-done = bf16[512,1024]{1,0:T(8,128)(2,1)} async-done(((bf16[2048,1024]{1,0:T(8,128)(2,1)}), bf16[512,1024]{1,0:T(8,128)(2,1)}) %reduce-scatter.11.cloned.1.call-update) | async-done | bytes 1048592 | tf_op jit(solution)/shard_map/reduce_scatter | solution.py:207
  745.1 39.5 %all-reduce.2 = (f32[2,1024]{1,0:T(2,128)}, f32[2,1024]{1,0:T(2,128)}) all-reduce(f32[2,1024]{1,0:T(2,128)S(1)} %get-tuple-element.59, f32[2,1024]{1,0:T(2,128)S(1)} %get-tuple-element.60), channel_id=1, replica_groups=mesh['dp'=8,'mp'=4] {'dp','mp'}, use_global_device_ids=true, to_apply=%region_33.34 | all-reduce | flops 4096 | bytes 32768 | tf_op jit(solution)/shard_map/psum | solution.py:222
  784.5 4.5 add_add_fusion.2
  (232 shorter events, 129.4 us)
Async XLA Ops:
  7.2 223.3 %copy-start = (bf16[1024,1024]{1,0:T(8,128)(2,1)S(1)}, bf16[1024,1024]{1,0:T(8,128)(2,1)}, u32[]{:S(2)}) copy-start(bf16[1024,1024]{1,0:T(8,128)(2,1)} %param.21) | copy-start | bytes 6291460
  7.2 14.5 %copy-start.48 = (bf16[2,256]{1,0:T(2,128)(2,1)S(1)}, bf16[2,256]{1,0:T(2,128)(2,1)}, u32[]{:S(2)}) copy-start(bf16[2,256]{1,0:T(2,128)(2,1)} %param.16) | copy-start | bytes 3076
  7.2 45.5 %all-gather.6.cloned.1.call-start = ((), (), s32[]{:S(2)}) async-start(), calls=%async_computation.4 | async-start | bytes 5242880 | tf_op jit(solution)/shard_map/all_gather | solution.py:133
  8.8 12.9 %copy-start.40 = (f32[512]{0:T(512)}, f32[512]{0:T(512)S(1)}, u32[]{:S(2)}) copy-start(f32[512]{0:T(512)S(1)} %broadcast_multiply_fusion.1) | copy-start | bytes 6148
  11.9 9.9 %copy-start.38 = (f32[1,1024]{1,0:T(1,128)}, f32[1,1024]{1,0:T(1,128)S(1)}, u32[]{:S(2)}) copy-start(f32[1,1024]{1,0:T(1,128)S(1)} %get-tuple-element.43) | copy-start | bytes 12292
  15.3 139.4 %reduce-scatter.5.cloned.1.call-start = ((), (), s32[]{:S(2)}) async-start(), calls=%async_computation.5 | async-start | bytes 5242880 | tf_op jit(solution)/shard_map/reduce_scatter | solution.py:145
  110.0 44.8 %copy-start.4 = (bf16[512,1024]{1,0:T(8,128)(2,1)S(1)}, bf16[512,1024]{1,0:T(8,128)(2,1)}, u32[]{:S(2)}) copy-start(bf16[512,1024]{1,0:T(8,128)(2,1)} %param.13) | copy-start | bytes 3145732
  110.0 84.5 %all-gather.8.cloned.1.call-start = ((), (), s32[]{:S(2)}) async-start(), calls=%async_computation.6 | async-start | bytes 5242880 | tf_op jit(solution)/shard_map/all_gather | solution.py:154
  159.9 70.5 %all-gather.10.cloned.1.call-start = ((), (), s32[]{:S(2)}) async-start(), calls=%async_computation.8 | async-start | bytes 5242880 | tf_op jit(solution)/shard_map/all_gather | solution.py:168
  160.5 150.5 %reduce-scatter.9.cloned.1.call-start = ((), (), s32[]{:S(2)}) async-start(), calls=%async_computation.9 | async-start | bytes 5242880 | tf_op jit(solution)/shard_map/reduce_scatter | solution.py:176
  230.5 29.5 %copy-start.54 = (bf16[1024,1024]{1,0:T(8,128)(2,1)S(1)}, bf16[1024,1024]{1,0:T(8,128)(2,1)}, u32[]{:S(2)}) copy-start(bf16[1024,1024]{1,0:T(8,128)(2,1)} %param.19) | copy-start | bytes 6291460
  266.2 91.7 %reduce-scatter.7.cloned.1.call-start = ((), (), s32[]{:S(2)}) async-start(), calls=%async_computation.7 | async-start | bytes 5242880 | tf_op jit(solution)/shard_map/reduce_scatter | solution.py:159
  285.1 25.9 %copy-start.7 = (bf16[512,1024]{1,0:T(8,128)(2,1)S(1)}, bf16[512,1024]{1,0:T(8,128)(2,1)}, u32[]{:S(2)}) copy-start(bf16[512,1024]{1,0:T(8,128)(2,1)} %reduce-scatter.5.cloned.1.call-done) | copy-start | bytes 3145732
  285.1 113.9 %all-gather.12.cloned.1.call-start = ((), (), s32[]{:S(2)}) async-start(), calls=%async_computation.10 | async-start | bytes 5242880 | tf_op jit(solution)/shard_map/all_gather | solution.py:186
  313.3 49.7 %copy-start.11 = (bf16[512,1024]{1,0:T(8,128)(2,1)S(1)}, bf16[512,1024]{1,0:T(8,128)(2,1)}, u32[]{:S(2)}) copy-start(bf16[512,1024]{1,0:T(8,128)(2,1)} %param.25) | copy-start | bytes 3145732
  364.3 330.0 %all-reduce.7.cloned.1.call-start = ((), (), s32[]{:S(2)}) async-start(), calls=%async_computation.12 | async-start | bytes 12582912 | tf_op jit(solution)/shard_map/psum | solution.py:213
  364.4 9.5 %copy-start.26 = (bf16[2048,1024]{1,0:T(8,128)(2,1)S(1)}, bf16[2048,1024]{1,0:T(8,128)(2,1)}, u32[]{:S(2)}) copy-start(bf16[2048,1024]{1,0:T(8,128)(2,1)} %all-gather.10.cloned.1.call-done) | copy-start | bytes 12582916
  364.4 9.5 %copy-start.28 = (bf16[2048,1024]{1,0:T(8,128)(2,1)S(1)}, bf16[2048,1024]{1,0:T(8,128)(2,1)}, u32[]{:S(2)}) copy-start(bf16[2048,1024]{1,0:T(8,128)(2,1)} %multiply_convert_fusion.2) | copy-start | bytes 12582916
  374.0 25.0 %copy-start.35 = (bf16[256,1024]{1,0:T(8,128)(2,1)S(1)}, bf16[256,1024]{1,0:T(8,128)(2,1)}, u32[]{:S(2)}) copy-start(bf16[256,1024]{1,0:T(8,128)(2,1)} %param.17) | copy-start | bytes 1572868
  410.4 10.5 %slice-start.4 = ((s8[8388608]{0:T(1024)(128)(4,1)}), s8[4194304]{0:T(1024)(128)(4,1)S(1)}, s32[]{:S(2)}) async-start(s8[8388608]{0:T(1024)(128)(4,1)} %bitcast.126), calls=%async_computation.17 | async-start | bytes 8388608
  429.6 14.7 %copy-start.20 = (bf16[2,512,4,64]{1,3,2,0:T(8,128)(2,1)S(1)}, bf16[2,512,4,64]{1,3,2,0:T(8,128)(2,1)}, u32[]{:S(2)}) copy-start(bf16[2,512,4,64]{1,3,2,0:T(8,128)(2,1)} %copy.98) | copy-start | bytes 1572868
  429.6 14.7 %copy-start.22 = (f32[2,512,4,64]{1,3,2,0:T(8,128)S(1)}, f32[2,512,4,64]{1,3,2,0:T(8,128)}, u32[]{:S(2)}) copy-start(f32[2,512,4,64]{1,3,2,0:T(8,128)} %fusion.42) | copy-start | bytes 3145732
  429.6 23.9 %slice-start = ((s8[16777216]{0:T(1024)(128)(4,1)}), s8[4194304]{0:T(1024)(128)(4,1)S(1)}, s32[]{:S(2)}) async-start(s8[16777216]{0:T(1024)(128)(4,1)} %bitcast.124), calls=%async_computation.13 | async-start | bytes 8388608
  429.6 23.9 %slice-start.1 = ((s8[16777216]{0:T(1024)(128)(4,1)}), s8[4194304]{0:T(1024)(128)(4,1)S(1)}, s32[]{:S(2)}) async-start(s8[16777216]{0:T(1024)(128)(4,1)} %bitcast.124), calls=%async_computation.14 | async-start | bytes 8388608
  429.6 23.9 %slice-start.2 = ((s8[16777216]{0:T(1024)(128)(4,1)}), s8[4194304]{0:T(1024)(128)(4,1)S(1)}, s32[]{:S(2)}) async-start(s8[16777216]{0:T(1024)(128)(4,1)} %bitcast.124), calls=%async_computation.15 | async-start | bytes 8388608
  453.5 21.8 %copy-start.23 = (bf16[32,8,2,1024]{3,1,2,0:T(8,128)(2,1)}, bf16[32,8,2,1024]{3,1,2,0:T(8,128)(2,1)S(1)}, u32[]{:S(2)}) copy-start(bf16[32,8,2,1024]{3,1,2,0:T(8,128)(2,1)S(1)} %copy.102) | copy-start | bytes 3145732
  483.1 257.4 %reduce-scatter.11.cloned.1.call-start = ((), (), s32[]{:S(2)}) async-start(), calls=%async_computation.11 | async-start | bytes 5242880 | tf_op jit(solution)/shard_map/reduce_scatter | solution.py:207
  702.4 38.1 %copy-start.39 = (f32[1,1024]{1,0:T(1,128)S(1)}, f32[1,1024]{1,0:T(1,128)}, u32[]{:S(2)}) copy-start(f32[1,1024]{1,0:T(1,128)} %copy-done.38) | copy-start | bytes 12292
  702.4 38.1 %copy-start.41 = (f32[512]{0:T(512)S(1)}, f32[512]{0:T(512)}, u32[]{:S(2)}) copy-start(f32[512]{0:T(512)} %copy-done.40) | copy-start | bytes 6148
  702.4 40.0 %copy-start.47 = (f32[512]{0:T(512)S(1)}, f32[512]{0:T(512)}, u32[]{:S(2)}) copy-start(f32[512]{0:T(512)} %copy-done.46) | copy-start | bytes 6148
  702.4 40.0 %copy-start.45 = (f32[512]{0:T(512)S(1)}, f32[512]{0:T(512)}, u32[]{:S(2)}) copy-start(f32[512]{0:T(512)} %copy-done.44) | copy-start | bytes 6148
  742.5 46.6 %copy-start.1 = (bf16[1024,1024]{1,0:T(8,128)(2,1)S(1)}, bf16[1024,1024]{1,0:T(8,128)(2,1)}, u32[]{:S(2)}) copy-start(bf16[1024,1024]{1,0:T(8,128)(2,1)} %param.21) | copy-start | bytes 6291460
  (39 other events, 131.2 us)
Sparse Core Ops, SparseCore 0:
  15.5 37.1 all-gather.5
  110.2 44.5 reduce-scatter.4
  160.0 34.4 all-gather.7
  196.0 34.4 all-gather.9
  266.4 44.5 reduce-scatter.8
  313.4 44.5 reduce-scatter.6
  364.5 34.4 all-gather.11
  483.2 211.0 all-reduce.6
  696.9 43.6 reduce-scatter.10
where the time goes:
time: 801 us; the launch traced here: 796 us
  waiting for transfers between devices  426 us (53%)
  matrix products  158 us (20%)
  other arithmetic  80 us (10%)
  blocking collectives  68.8 us (9%)
  local copies, waits for them, and re-layouts  47.6 us (6%)
  between operations  14.9 us (2%)
    psum x1, waiting for transfers between devices, shards(): lax.psum(grad_qkv.astype(jnp.bfloat16), 'dp').astype(jnp.float32)  171 us
    reduce_scatter x1, waiting for transfers between devices, shards(): lax.psum_scatter(jnp.dot(activ, w_down, preferred_element_type=jnp.float3...  44.7 us
    reduce_scatter x1, waiting for transfers between devices, shards(): lax.psum_scatter(jnp.dot(attended, w_out, preferred_element_type=jnp.floa...  44.1 us
    psum x1, blocking collectives, shards(): lax.psum((jnp.stack([grad_g1, grad_g2]), jnp.stack([grad_s1, grad_s2])),...  39.5 us
    reduce_scatter x1, waiting for transfers between devices, shards(): lax.psum_scatter(summed.astype(jnp.bfloat16), 'mp', scatter_dimension=0,...  35.1 us
    all_gather x1, waiting for transfers between devices, shards(): joined2 = lax.all_gather(lowered2, 'mp', axis=0, tiled=True)  34 us
    dot_general x1, matrix products, shards(): jnp.einsum('td,fd->tf', grad_z, w_down, preferred_element_type=jnp.float32)  27.5 us
    all_gather x1, waiting for transfers between devices, shards(): lax.all_gather(lowered, 'mp', axis=0, tiled=True)  27.5 us
  transfers between devices with their start and end apart: 9, of which 9 were waited for; matrix products, arithmetic and copies ran while one was open for 10% of the time, Pallas kernels for 0%

commit v1 on v0

--- a/solution.py
+++ b/solution.py
@@ -7,6 +7,19 @@
 LEN = 1024
 QBLK = 512
 EPS = 1e-05
+
+
+def ring_gather(x, axis, dim):
+    ways = lax.axis_size(axis)
+    up = [(d, (d + 1) % ways) for d in range(ways)]
+    down = [(d, (d - 1) % ways) for d in range(ways)]
+    earlier, later = ([x], [x])
+    for _ in range(ways // 2):
+        earlier.append(lax.ppermute(earlier[-1], axis, up))
+    for _ in range((ways - 1) // 2):
+        later.append(lax.ppermute(later[-1], axis, down))
+    line = jnp.concatenate([*earlier[::-1], *later[1:]], axis=dim)
+    return jnp.roll(line, (lax.axis_index(axis) - ways // 2) * x.shape[dim], axis=dim)
 
 
 def norm_rows(values, gain, shift):
@@ -130,7 +143,7 @@
     normed, first_back = jax.vjp(norm_rows, resid, ln_gain[0], ln_bias[0])
     lowered = normed.astype(jnp.bfloat16)
     joined, seg_all = (
-        lax.all_gather(lowered, "mp", axis=0, tiled=True),
+        ring_gather(lowered, "mp", 0),
         lax.all_gather(segment_ids, "mp", axis=0, tiled=True),
     )
     query = (jnp.dot(joined, w_qkv[0], preferred_element_type=jnp.float32) + qv_bias[0]).astype(

time: 801 us -> 824 us (1.029)
  local copies, waits for them, and re-layouts: 47.6 us -> 65.7 us
    all_gather x1 -> x0, waiting for transfers between devices: 27.5 us -> none  [shards(): lax.all_gather(lowered, 'mp', axis=0, tiled=True)]
    ppermute x0 -> x3, waiting for transfers between devices: none -> 20.2 us  [the longest x2 20.2 us: ring_gather(): earlier.append(lax.ppermute(earlier[-1], axis, up))]
    reshape x6, local copies, waits for them, and re-layouts: 15.9 us -> 24.8 us  [split_heads(): return flat.reshape(rows, LEN, flat.shape[1] // HD, HD)]
    unnamed x132 -> x143, local copies, waits for them, and re-layouts: 20.4 us -> 27.9 us
  transfers between devices with their start and end apart: 9 -> 11, of which waited for: 9 -> 9; matrix products, arithmetic and copies ran while one was open for 10% -> 10% of each run, Pallas kernels for 0% -> 0%
where the time goes in v1:
time: 824 us; the launch traced here: 816 us
  waiting for transfers between devices  423 us (51%)
  matrix products  151 us (18%)
  other arithmetic  80.2 us (10%)
  blocking collectives  75.4 us (9%)
  local copies, waits for them, and re-layouts  65.7 us (8%)
  between operations  15.2 us (2%)
    psum x1, waiting for transfers between devices, shards(): lax.psum(grad_qkv.astype(jnp.bfloat16), 'dp').astype(jnp.float32)  171 us
    reduce_scatter x1, waiting for transfers between devices, shards(): lax.psum_scatter(jnp.dot(attended, w_out, preferred_element_type=jnp.floa...  47.9 us
    reduce_scatter x1, waiting for transfers between devices, shards(): lax.psum_scatter(jnp.dot(activ, w_down, preferred_element_type=jnp.float3...  44.7 us
    psum x1, blocking collectives, shards(): lax.psum((jnp.stack([grad_g1, grad_g2]), jnp.stack([grad_s1, grad_s2])),...  39.5 us
    reduce_scatter x1, waiting for transfers between devices, shards(): lax.psum_scatter(summed.astype(jnp.bfloat16), 'mp', scatter_dimension=0,...  35.1 us
    all_gather x1, waiting for transfers between devices, shards(): joined2 = lax.all_gather(lowered2, 'mp', axis=0, tiled=True)  33.8 us
    unnamed x143, local copies, waits for them, and re-layouts  27.9 us
    dot_general x1, matrix products, shards(): jnp.einsum('td,fd->tf', grad_z, w_down, preferred_element_type=jnp.float32)  27.4 us
  transfers between devices with their start and end apart: 11, of which 9 were waited for; matrix products, arithmetic and copies ran while one was open for 10% of the time, Pallas kernels for 0%

profile of v1, /device:TPU:0, one launch (start us, length us, event | category | flops | bytes accessed | tf_op | source)
XLA Modules:
  0.0 816.3 jit_solution(717516989512918069)
XLA Ops:
  18.4 20.2 %collective-permute-done = bf16[512,1024]{1,0:T(8,128)(2,1)} collective-permute-done((bf16[512,1024]{1,0:T(8,128)(2,1)}, bf16[512,1024]{1,0:T(8,128)(2,1)}, u32[]{:S(2)}, u32[]{:S(2)}) %collective-permute-start) | collective-permute-done | bytes 1048608 | tf_op jit(solution)/shard_map/ppermute | solution.py:18
  41.1 12.8 %all-gather = s32[4,1,512]{2,1,0:T(1,128)S(1)} all-gather(s32[1,1,512]{2,1,0:T(1,128)S(1)} %bitcast.163), channel_id=1, replica_groups=mesh['dp'=8,'mp'=4] {'mp'}, dimensions={0}, use_global_device_ids=true | all-gather | bytes 10240 | tf_op jit(solution)/shard_map/all_gather | solution.py:147
  74.3 4.6 reshape.219
  78.8 4.0 copy.62
  82.9 4.4 reshape.220
  95.4 4.4 reshape.221
  99.8 4.1 copy.66
  131.6 47.9 %reduce-scatter.5.cloned.1.call-done = bf16[512,1024]{1,0:T(8,128)(2,1)} async-done(((bf16[2048,1024]{1,0:T(8,128)(2,1)}), bf16[512,1024]{1,0:T(8,128)(2,1)}) %reduce-scatter.5.cloned.1.call-update) | async-done | bytes 1048592 | tf_op jit(solution)/shard_map/reduce_scatter | solution.py:158
  185.4 33.8 %all-gather.5.cloned.1.call-done = bf16[2048,1024]{1,0:T(8,128)(2,1)} async-done(((bf16[512,1024]{1,0:T(8,128)(2,1)}), bf16[2048,1024]{1,0:T(8,128)(2,1)}) %all-gather.5.cloned.1.call-update) | async-done | bytes 4194320 | tf_op jit(solution)/shard_map/all_gather | solution.py:167
  219.2 11.4 %fusion.121 = f32[2048,1024]{1,0:T(8,128)} fusion(bf16[2048,1024]{1,0:T(8,128)(2,1)} %all-gather.5.cloned.1.call-done, bf16[1024,1024]{1,0:T(8,128)(2,1)} %param.19), kind=kOutput, calls=%fused_computation.186 | convolution fusion | flops 4294967296 | bytes 14680064 | tf_op jit(solution)/shard_map/dot_general | solution.py:168
  230.6 24.7 %all-gather.7.cloned.1.call-done = bf16[2048,1024]{1,0:T(8,128)(2,1)} async-done(((bf16[512,1024]{1,0:T(8,128)(2,1)}), bf16[2048,1024]{1,0:T(8,128)(2,1)}) %all-gather.7.cloned.1.call-update) | async-done | bytes 4194320 | tf_op jit(solution)/shard_map/all_gather | solution.py:181
  255.3 27.4 %fusion.108 = (bf16[1024]{0:T(1024)(128)(2,1)S(1)}, bf16[2048,1024]{1,0:T(8,128)(2,1)S(1)}, f32[2048,1024]{1,0:T(8,128)}) fusion(f32[2048,1024]{1,0:T(8,128)} %fusion.121, f32[1024]{0:T(1024)S(1)} %convert_element_type.188, bf16[2048,1024]{1,0:T(8,128)(2,1)} %all-gather.7.cloned.1.call-done, bf16[1024,1024]{1,0:T(8,128)(2,1)S(1)} %copy-done), kind=kOutput, calls=%fused_computation.174 | convolution fusion | flops 4450155520 | bytes 27269120 | tf_op jit(solution)/shard_map/td,fd->tf/dot_general | solution.py:184
  284.7 6.2 convolution_convert_fusion.1
  291.0 10.4 %multiply_convert_fusion.2 = bf16[2048,1024]{1,0:T(8,128)(2,1)} fusion(f32[2048,1024]{1,0:T(8,128)} %get-tuple-element.31, f32[2048,1024]{1,0:T(8,128)} %fusion.121, f32[1024]{0:T(1024)S(1)} %convert_element_type.188), kind=kLoop, calls=%fused_computation.17 | loop fusion | flops 8388608 | bytes 20975616 | tf_op jit(solution)/shard_map/convert_element_type | solution.py:169
  301.4 8.4 %convolution_convert_fusion.2 = bf16[2048,1024]{1,0:T(8,128)(2,1)} fusion(bf16[2048,1024]{1,0:T(8,128)(2,1)} %multiply_convert_fusion.2, bf16[1024,1024]{1,0:T(8,128)(2,1)S(1)} %copy-done), kind=kOutput, calls=%fused_computation.43 | convolution fusion | flops 4297064448 | bytes 10485760 | tf_op jit(solution)/shard_map/dot_general | solution.py:173
  310.4 25.2 %reduce-scatter.9.cloned.1.call-done = bf16[512,1024]{1,0:T(8,128)(2,1)} async-done(((bf16[2048,1024]{1,0:T(8,128)(2,1)}), bf16[512,1024]{1,0:T(8,128)(2,1)}) %reduce-scatter.9.cloned.1.call-update) | async-done | bytes 1048592 | tf_op jit(solution)/shard_map/reduce_scatter | solution.py:189
  338.0 44.7 %reduce-scatter.7.cloned.1.call-done = bf16[512,1024]{1,0:T(8,128)(2,1)} async-done(((bf16[2048,1024]{1,0:T(8,128)(2,1)}), bf16[512,1024]{1,0:T(8,128)(2,1)}) %reduce-scatter.7.cloned.1.call-update) | async-done | bytes 1048592 | tf_op jit(solution)/shard_map/reduce_scatter | solution.py:172
  389.1 9.5 %convolution_convert_fusion.6 = bf16[1024,1024]{1,0:T(8,128)(2,1)} fusion(bf16[2048,1024]{1,0:T(8,128)(2,1)} %all-gather.5.cloned.1.call-done, bf16[2048,1024]{1,0:T(8,128)(2,1)} %copy-done.56), kind=kOutput, calls=%fused_computation.90 | convolution fusion | flops 4296015872 | bytes 10485760 | tf_op jit(solution)/shard_map/td,tf->df/dot_general | solution.py:187
  398.6 6.0 convolution_convert_fusion.5
  404.6 19.0 %all-gather.9.cloned.1.call-done = bf16[2048,1024]{1,0:T(8,128)(2,1)} async-done(((bf16[512,1024]{1,0:T(8,128)(2,1)}), bf16[2048,1024]{1,0:T(8,128)(2,1)}) %all-gather.9.cloned.1.call-update) | async-done | bytes 4194320 | tf_op jit(solution)/shard_map/all_gather | solution.py:199
  423.6 4.4 convolution_convert_fusion.3
  435.0 5.9 fusion.51
  440.9 4.6 multiply_reduce_fusion.1
  454.2 12.4 %multiply_reduce_fusion = (f32[2,4,512]{2,1,0:T(4,128)S(1)}, f32[2,4,512,1024]{3,2,1,0:T(8,128)}) fusion(f32[2,4,512,1024]{3,2,1,0:T(8,128)} %copy-done.2, f32[2,4,512]{2,1,0:T(4,128)S(1)} %bitcast.134, bf16[2,512,4,64]{1,3,2,0:T(8,128)(2,1)} %copy.98, bf16[2,1024,4,64]{1,3,2,0:T(8,128)(2,1)S(1)} %copy-done.14), kind=kOutput, calls=%fused_computation.1 | convolution fusion | flops 549449728 | bytes 35160064 | tf_op jit(solution)/shard_map/rqhd,rkhd->rhqk/dot_general | solution.py:92
  466.7 7.7 fusion.120
  475.7 4.8 fusion.70
  480.6 8.1 multiply_convert_fusion
  517.7 23.1 %all-reduce.3 = (bf16[2,256]{1,0:T(2,128)(2,1)S(1)}, bf16[1024]{0:T(1024)(128)(2,1)S(1)}, bf16[1024]{0:T(1024)(128)(2,1)S(1)}, bf16[1024]{0:T(1024)(128)(2,1)S(1)}) all-reduce(bf16[2,256]{1,0:T(2,128)(2,1)S(1)} %pad_maximum_fusion.4, bf16[1024]{0:T(1024)(128)(2,1)S(1)} %reduce_sum.244, ...), channel_id=1, replica_groups=mesh['dp'=8,'mp'=4] {'dp'}, use_global_device_ids=true, to_apply=%region_21.22 | all-reduce | flops 3584 | bytes 14336 | tf_op jit(solution)/shard_map/psum | solution.py:227
  543.1 171.4 %all-reduce.7.cloned.1.call-done = (bf16[3,1024,256]{2,1,0:T(8,128)(2,1)}, bf16[256,1024]{1,0:T(8,128)(2,1)}, bf16[1024,1024]{1,0:T(8,128)(2,1)}, bf16[1024,1024]{1,0:T(8,128)(2,1)}) async-done(((bf16[3,1024,256]{2,1,0:T(8,128)(2,1)}, bf16[256,1024]{1,0:T(8,128)(2,1)}, bf16[1024,1024]{1,0:T(8,128)(2,1)}, bf16[1024,1024]{1,0:T(8,128)(2,1)}), (bf16[3,1024,256]{2,1,0:T(8,128)(2,1)}, ...) | async-done | bytes 6291472 | tf_op jit(solution)/shard_map/psum | solution.py:226
  725.6 35.1 %reduce-scatter.11.cloned.1.call-done = bf16[512,1024]{1,0:T(8,128)(2,1)} async-done(((bf16[2048,1024]{1,0:T(8,128)(2,1)}), bf16[512,1024]{1,0:T(8,128)(2,1)}) %reduce-scatter.11.cloned.1.call-update) | async-done | bytes 1048592 | tf_op jit(solution)/shard_map/reduce_scatter | solution.py:220
  765.3 39.5 %all-reduce.2 = (f32[2,1024]{1,0:T(2,128)}, f32[2,1024]{1,0:T(2,128)}) all-reduce(f32[2,1024]{1,0:T(2,128)S(1)} %get-tuple-element.59, f32[2,1024]{1,0:T(2,128)S(1)} %get-tuple-element.60), channel_id=1, replica_groups=mesh['dp'=8,'mp'=4] {'dp','mp'}, use_global_device_ids=true, to_apply=%region_33.34 | all-reduce | flops 4096 | bytes 32768 | tf_op jit(solution)/shard_map/psum | solution.py:235
  804.7 4.5 add_add_fusion.2
  (250 shorter events, 150.4 us)
Async XLA Ops:
  7.2 248.1 %copy-start = (bf16[1024,1024]{1,0:T(8,128)(2,1)S(1)}, bf16[1024,1024]{1,0:T(8,128)(2,1)}, u32[]{:S(2)}) copy-start(bf16[1024,1024]{1,0:T(8,128)(2,1)} %param.21) | copy-start | bytes 6291460
  7.2 33.9 %copy-start.51 = (s32[512]{0:T(512)S(1)}, s32[512]{0:T(512)}, u32[]{:S(2)}) copy-start(s32[512]{0:T(512)} %param.14) | copy-start | bytes 6148
  7.2 48.1 %copy-start.50 = (bf16[2,256]{1,0:T(2,128)(2,1)S(1)}, bf16[2,256]{1,0:T(2,128)(2,1)}, u32[]{:S(2)}) copy-start(bf16[2,256]{1,0:T(2,128)(2,1)} %param.16) | copy-start | bytes 3076
  7.2 172.2 %reduce-scatter.5.cloned.1.call-start = ((), (), s32[]{:S(2)}) async-start(), calls=%async_computation.4 | async-start | bytes 5242880 | tf_op jit(solution)/shard_map/reduce_scatter | solution.py:158
  8.8 56.4 %copy-start.42 = (f32[512]{0:T(512)}, f32[512]{0:T(512)S(1)}, u32[]{:S(2)}) copy-start(f32[512]{0:T(512)S(1)} %broadcast_multiply_fusion.1) | copy-start | bytes 6148
  10.5 30.6 %copy-start.48 = (f32[512]{0:T(512)}, f32[512]{0:T(512)S(1)}, u32[]{:S(2)}) copy-start(f32[512]{0:T(512)S(1)} %fusion.31) | copy-start | bytes 6148
  10.5 54.7 %copy-start.44 = (f32[512]{0:T(512)}, f32[512]{0:T(512)S(1)}, u32[]{:S(2)}) copy-start(f32[512]{0:T(512)S(1)} %fusion.100) | copy-start | bytes 6148
  11.3 53.9 %copy-start.37 = (f32[1,1024]{1,0:T(1,128)}, f32[1,1024]{1,0:T(1,128)S(1)}, u32[]{:S(2)}) copy-start(f32[1,1024]{1,0:T(1,128)S(1)} %get-tuple-element.43) | copy-start | bytes 12292
  14.7 46.0 %copy-start.4 = (bf16[512,1024]{1,0:T(8,128)(2,1)S(1)}, bf16[512,1024]{1,0:T(8,128)(2,1)}, u32[]{:S(2)}) copy-start(bf16[512,1024]{1,0:T(8,128)(2,1)} %param.13) | copy-start | bytes 3145732
  14.7 23.8 %collective-permute-start = (bf16[512,1024]{1,0:T(8,128)(2,1)}, bf16[512,1024]{1,0:T(8,128)(2,1)}, u32[]{:S(2)}, u32[]{:S(2)}) collective-permute-start(bf16[512,1024]{1,0:T(8,128)(2,1)} %fusion.29), channel_id=1, source_target_pairs={{0,1},{1,2},{2,3},{3,0},{4,5},{5,6},{6,7},{7,4},{8,9},{9,10},{10,1... | collective-permute-start | bytes 3145736 | tf_op jit(solution)/shard_map/ppermute | solution.py:18
  15.2 45.9 %collective-permute-start.2 = (bf16[512,1024]{1,0:T(8,128)(2,1)}, bf16[512,1024]{1,0:T(8,128)(2,1)}, u32[]{:S(2)}, u32[]{:S(2)}) collective-permute-start(bf16[512,1024]{1,0:T(8,128)(2,1)} %fusion.29), channel_id=1, source_target_pairs={{0,3},{1,0},{2,1},{3,2},{4,7},{5,4},{6,5},{7,6},{8,11},{9,8},{10,9... | collective-permute-start | bytes 3145736 | tf_op jit(solution)/shard_map/ppermute | solution.py:20
  38.6 19.5 %collective-permute-start.1 = (bf16[512,1024]{1,0:T(8,128)(2,1)}, bf16[512,1024]{1,0:T(8,128)(2,1)}, u32[]{:S(2)}, u32[]{:S(2)}) collective-permute-start(bf16[512,1024]{1,0:T(8,128)(2,1)} %collective-permute-done), channel_id=1, source_target_pairs={{0,1},{1,2},{2,3},{3,0},{4,5},{5,6},{6,7},{7,4},{8,9},{9,10},{10,1... | collective-permute-start | bytes 3145736 | tf_op jit(solution)/shard_map/ppermute | solution.py:18
  130.9 88.3 %all-gather.5.cloned.1.call-start = ((), (), s32[]{:S(2)}) async-start(), calls=%async_computation.5 | async-start | bytes 5242880 | tf_op jit(solution)/shard_map/all_gather | solution.py:167
  184.6 70.7 %all-gather.7.cloned.1.call-start = ((), (), s32[]{:S(2)}) async-start(), calls=%async_computation.7 | async-start | bytes 5242880 | tf_op jit(solution)/shard_map/all_gather | solution.py:181
  185.3 150.3 %reduce-scatter.9.cloned.1.call-start = ((), (), s32[]{:S(2)}) async-start(), calls=%async_computation.8 | async-start | bytes 5242880 | tf_op jit(solution)/shard_map/reduce_scatter | solution.py:189
  255.3 29.4 %copy-start.55 = (bf16[1024,1024]{1,0:T(8,128)(2,1)S(1)}, bf16[1024,1024]{1,0:T(8,128)(2,1)}, u32[]{:S(2)}) copy-start(bf16[1024,1024]{1,0:T(8,128)(2,1)} %param.19) | copy-start | bytes 6291460
  290.9 91.7 %reduce-scatter.7.cloned.1.call-start = ((), (), s32[]{:S(2)}) async-start(), calls=%async_computation.6 | async-start | bytes 5242880 | tf_op jit(solution)/shard_map/reduce_scatter | solution.py:172
  309.8 25.9 %copy-start.6 = (bf16[512,1024]{1,0:T(8,128)(2,1)S(1)}, bf16[512,1024]{1,0:T(8,128)(2,1)}, u32[]{:S(2)}) copy-start(bf16[512,1024]{1,0:T(8,128)(2,1)} %reduce-scatter.5.cloned.1.call-done) | copy-start | bytes 3145732
  309.8 113.8 %all-gather.9.cloned.1.call-start = ((), (), s32[]{:S(2)}) async-start(), calls=%async_computation.9 | async-start | bytes 5242880 | tf_op jit(solution)/shard_map/all_gather | solution.py:199
  337.9 49.7 %copy-start.10 = (bf16[512,1024]{1,0:T(8,128)(2,1)S(1)}, bf16[512,1024]{1,0:T(8,128)(2,1)}, u32[]{:S(2)}) copy-start(bf16[512,1024]{1,0:T(8,128)(2,1)} %param.25) | copy-start | bytes 3145732
  389.0 325.6 %all-reduce.7.cloned.1.call-start = ((), (), s32[]{:S(2)}) async-start(), calls=%async_computation.11 | async-start | bytes 12582912 | tf_op jit(solution)/shard_map/psum | solution.py:226
  398.6 25.0 %copy-start.35 = (bf16[256,1024]{1,0:T(8,128)(2,1)S(1)}, bf16[256,1024]{1,0:T(8,128)(2,1)}, u32[]{:S(2)}) copy-start(bf16[256,1024]{1,0:T(8,128)(2,1)} %param.17) | copy-start | bytes 1572868
  454.2 12.4 %copy-start.21 = (f32[2,512,4,64]{1,3,2,0:T(8,128)S(1)}, f32[2,512,4,64]{1,3,2,0:T(8,128)}, u32[]{:S(2)}) copy-start(f32[2,512,4,64]{1,3,2,0:T(8,128)} %fusion.51) | copy-start | bytes 3145732
  466.7 13.9 %slice-start = ((s8[16777216]{0:T(1024)(128)(4,1)}), s8[4194304]{0:T(1024)(128)(4,1)S(1)}, s32[]{:S(2)}) async-start(s8[16777216]{0:T(1024)(128)(4,1)} %bitcast.118), calls=%async_computation.12 | async-start | bytes 8388608
  466.7 13.9 %slice-start.1 = ((s8[16777216]{0:T(1024)(128)(4,1)}), s8[4194304]{0:T(1024)(128)(4,1)S(1)}, s32[]{:S(2)}) async-start(s8[16777216]{0:T(1024)(128)(4,1)} %bitcast.118), calls=%async_computation.13 | async-start | bytes 8388608
  466.7 13.9 %slice-start.2 = ((s8[16777216]{0:T(1024)(128)(4,1)}), s8[4194304]{0:T(1024)(128)(4,1)S(1)}, s32[]{:S(2)}) async-start(s8[16777216]{0:T(1024)(128)(4,1)} %bitcast.118), calls=%async_computation.14 | async-start | bytes 8388608
  503.3 257.4 %reduce-scatter.11.cloned.1.call-start = ((), (), s32[]{:S(2)}) async-start(), calls=%async_computation.10 | async-start | bytes 5242880 | tf_op jit(solution)/shard_map/reduce_scatter | solution.py:220
  722.6 38.1 %copy-start.38 = (f32[1,1024]{1,0:T(1,128)S(1)}, f32[1,1024]{1,0:T(1,128)}, u32[]{:S(2)}) copy-start(f32[1,1024]{1,0:T(1,128)} %copy-done.37) | copy-start | bytes 12292
  722.6 38.1 %copy-start.43 = (f32[512]{0:T(512)S(1)}, f32[512]{0:T(512)}, u32[]{:S(2)}) copy-start(f32[512]{0:T(512)} %copy-done.42) | copy-start | bytes 6148
  722.6 40.0 %copy-start.49 = (f32[512]{0:T(512)S(1)}, f32[512]{0:T(512)}, u32[]{:S(2)}) copy-start(f32[512]{0:T(512)} %copy-done.48) | copy-start | bytes 6148
  722.6 40.0 %copy-start.45 = (f32[512]{0:T(512)S(1)}, f32[512]{0:T(512)}, u32[]{:S(2)}) copy-start(f32[512]{0:T(512)} %copy-done.44) | copy-start | bytes 6148
  762.7 46.6 %copy-start.1 = (bf16[1024,1024]{1,0:T(8,128)(2,1)S(1)}, bf16[1024,1024]{1,0:T(8,128)(2,1)}, u32[]{:S(2)}) copy-start(bf16[1024,1024]{1,0:T(8,128)(2,1)} %param.21) | copy-start | bytes 6291460
  (44 other events, 159.7 us)
Sparse Core Ops, SparseCore 0:
  131.0 48.3 reduce-scatter.4
  184.7 34.4 all-gather.4
  220.8 34.4 all-gather.6
  291.0 44.5 reduce-scatter.8
  338.0 44.5 reduce-scatter.6
  389.1 34.4 all-gather.8
  503.4 211.0 all-reduce.6
  717.1 43.6 reduce-scatter.10
